TPU v7x, 32 devices: a whole 2x2x4 slice. The times are simulated.
32 devices in a mesh: lon: 8 (over y, x, core), lat: 4 (over z).
Axes of the slice: x: 2, y: 2, z: 4, core: 2. Of those that a mesh axis runs over, the one named last changes fastest.
Arguments:
- gradient: float32 [137, 16, 1024], P(None, 'lat', 'lon'), may hold values from -60 to 60
- obs_weight: float32 [137, 16, 1024], P(None, 'lat', 'lon'), may hold values from 0.2 to 5
- half_width: int32 [16], P('lat'), may hold values from 8 to 32
- zonal_coef: float32 [16, 33], P('lat'), may hold values from 0.2 to 1
- mirror_map: int32 [1024], P('lon'), may hold values from 0 to 1023, as said below
- merid_coef: float32 [5], replicated, may hold values from 0.2 to 1
- vertical_map: float32 [137, 137], replicated, may hold values from -0.5 to 0.5
Outputs:
- increment: float32 [137, 16, 1024], P(None, 'lat', 'lon')
- residual: float32 [137, 16, 1024], P(None, 'lat', 'lon')
Inputs may be any that keep to these rules, and one draw needn't show every extreme that they name: mirror_map[mirror_map[i]] = i, and mirror_map[i] lies in the block of 128 longitudes whose block index differs from i // 128 by 4.
All inputs are finite; a program needn't handle non-finite values.
Results may differ from a plain program's by a relative error of at most 0.04.
Values sent between devices are 32-bit elements; how exact they have to be, the bound alone decides.
No kernel may reach another device: no remote copies, remote signals or barrier semaphores. Data moves between devices by JAX's collectives and lax.ppermute only.
A program may use at most 64 MiB of HBM per device.

v0:
```python
import jax
import jax.numpy as jnp
from jax import lax
from jax.sharding import PartitionSpec as P

OUTER = 2


def extended_2(block, sides, width, periodic):
    for axis, dim in sides:
        count = lax.axis_size(axis)
        forward = [(i, i + 1) for i in range(count - 1)]
        if periodic:
            forward.append((count - 1, 0))
        backward = [(target, source) for source, target in forward]
        low = lax.ppermute(
            lax.slice_in_dim(block, block.shape[dim] - width, None, axis=dim), axis, forward
        )
        high = lax.ppermute(lax.slice_in_dim(block, 0, width, axis=dim), axis, backward)
        block = jnp.concatenate([low, block, high], axis=dim)
    return block


def from_partner(value, axis, distance):
    return lax.ppermute(value, axis, [(i, i ^ 1 << distance) for i in range(lax.axis_size(axis))])


def zonal_weights(half_width, zonal_coef):
    tap_ids = jnp.arange(zonal_coef.shape[1], dtype=jnp.int32)
    kept = jnp.where(
        tap_ids[None, :] <= half_width[:, None], zonal_coef, jnp.zeros_like(zonal_coef)
    )
    scaling = jnp.sqrt(kept[:, 0] ** 2 + 2.0 * jnp.sum(kept[:, 1:] ** 2, axis=1))
    return kept / scaling[:, None]


def merid_weights(merid_coef):
    norm_value = jnp.sqrt(merid_coef[0] ** 2 + 2.0 * jnp.sum(merid_coef[1:] ** 2))
    return merid_coef / norm_value


def zonal_tables(weights, lon_dev):
    width = weights.shape[1] - 1
    positions = jnp.arange(lon_dev + 2 * width, dtype=jnp.int32)
    columns = jnp.arange(lon_dev, dtype=jnp.int32)
    tap_ids = jnp.arange(width + 1, dtype=jnp.int32)
    distance = jnp.abs(positions[:, None] - width - columns[None, :])
    selector = (distance[:, :, None] == tap_ids[None, None, :]).astype(jnp.float32)
    return jnp.einsum("pct,jt->jpc", selector, weights, precision=lax.Precision.HIGHEST)


def zonal_apply(padded, table):
    return jnp.einsum("ljp,jpc->ljc", padded, table, precision=lax.Precision.HIGHEST)


def lon_rim(field_in, width):
    return extended_2(field_in, (("lon", 2),), width, True)


def edge_rows(field_in):
    return jnp.concatenate([field_in, field_in], axis=1)


def merid_apply(field_in, polar, mirror_local, weights):
    rim_depth = weights.shape[0] - 1
    row_count = field_in.shape[1]
    extended = extended_2(field_in, (("lat", 1),), rim_depth, False)
    mirrored = jnp.take(polar, mirror_local, axis=2)
    north_rows = jnp.flip(mirrored[:, :rim_depth], axis=1)
    south_rows = jnp.flip(mirrored[:, rim_depth:], axis=1)
    band_index = lax.axis_index("lat")
    band_count = lax.axis_size("lat")
    upper_rim = jnp.where(band_index == 0, north_rows, extended[:, :rim_depth])
    lower_rim = jnp.where(
        band_index == band_count - 1, south_rows, extended[:, rim_depth + row_count :]
    )
    full_rows = jnp.concatenate([upper_rim, field_in, lower_rim], axis=1)
    result = weights[0] * field_in
    for offset in range(1, rim_depth + 1):
        upper = full_rows[:, rim_depth - offset : rim_depth - offset + row_count]
        lower = full_rows[:, rim_depth + offset : rim_depth + offset + row_count]
        result = result + weights[offset] * (upper + lower)
    return result


def per_device(gradient, obs_weight, half_width, zonal_coef, mirror_map, merid_coef, vertical_map):
    width = zonal_coef.shape[1] - 1
    lon_dev = gradient.shape[2]
    zonal_w = zonal_weights(half_width, zonal_coef)
    merid_w = merid_weights(merid_coef)
    table = zonal_tables(zonal_w, lon_dev)
    mirror_local = mirror_map % lon_dev
    partner_bit = lax.axis_size("lon").bit_length() - 2

    def hessian(vector):
        padded = lon_rim(vector, width)
        zonal_out = zonal_apply(padded, table)
        polar = from_partner(edge_rows(zonal_out), "lon", partner_bit)
        forward = merid_apply(zonal_out, polar, mirror_local, merid_w)
        lifted = jnp.einsum("kl,lji->kji", vertical_map, forward, precision=lax.Precision.HIGHEST)
        lowered = jnp.einsum(
            "lk,lji->kji", vertical_map, obs_weight * lifted, precision=lax.Precision.HIGHEST
        )
        returned = from_partner(edge_rows(lowered), "lon", partner_bit)
        merid_back = merid_apply(lowered, returned, mirror_local, merid_w)
        back = zonal_apply(lon_rim(merid_back, width), table)
        return vector + back

    increment = jnp.zeros_like(gradient)
    residual = gradient
    for outer in range(OUTER):
        first = hessian(residual)
        sum_rr, sum_rf, sum_ff = lax.psum(
            (jnp.sum(residual * residual), jnp.sum(residual * first), jnp.sum(first * first)),
            ("lon", "lat"),
        )
        second = hessian(first)
        sum_fs = lax.psum(jnp.sum(first * second), ("lon", "lat"))
        determinant = sum_rf * sum_fs - sum_ff * sum_ff
        coef_one = (sum_fs * sum_rr - sum_ff * sum_rf) / determinant
        coef_two = (sum_rf * sum_rf - sum_ff * sum_rr) / determinant
        increment = increment + coef_one * residual + coef_two * first
        residual = residual - coef_one * first - coef_two * second
    return (increment, residual)


def solution(mesh):
    placed = (
        P(None, "lat", "lon"),
        P(None, "lat", "lon"),
        P("lat"),
        P("lat", None),
        P("lon"),
        P(),
        P(),
    )
    return jax.shard_map(
        per_device,
        mesh=mesh,
        in_specs=placed,
        out_specs=(P(None, "lat", "lon"), P(None, "lat", "lon")),
        check_vma=False,
    )
```

profile of v0, /device:TPU:0, one launch (start us, length us, event | category | flops | bytes accessed | tf_op | source)
XLA Modules:
  0.0 374.2 jit_solution(15704041245719016282)
XLA Ops:
  2.3 2.9 collective-permute-start.1
  5.9 1.3 fusion
  8.6 1.5 collective-permute-done
  10.1 1.5 collective-permute-done.1
  12.7 2.7 collective-permute-start.2
  16.1 4.2 %collective-permute-start.3 = (f32[137,4,128]{2,0,1:T(8,128)S(1)}, f32[137,4,128]{2,0,1:T(8,128)}, u32[]{:S(2)}, u32[]{:S(2)}) collective-permute-start(f32[137,4,128]{2,0,1:T(8,128)S(1)} %convolution_bitcast_fusion.15), channel_id=1, source_target_pairs={{0,1},{1,2},{2,3},{4,5},{5,6},{6,7},{8,9},{9,10},{10,11},{12,13},{... | collective-permute-start | bytes 841736 | tf_op jit(solution)/shard_map/ppermute | solution.py:16
  20.3 1.3 collective-permute-start.4
  21.6 7.2 %collective-permute-done.2 = f32[137,8,128]{2,1,0:T(8,128)S(1)} collective-permute-done((f32[137,8,128]{2,1,0:T(8,128)S(1)}, f32[137,8,128]{2,1,0:T(8,128)S(1)}, u32[]{:S(2)}, u32[]{:S(2)}) %collective-permute-start.2) | collective-permute-done | bytes 561184 | tf_op jit(solution)/shard_map/ppermute | solution.py:25
  31.7 3.9 %fusion.5 = f32[137,4,128]{2,0,1:T(8,128)S(1)} fusion(f32[137,4,128]{2,0,1:T(8,128)S(1)} %reverse_select_fusion.14, f32[137,4,128]{2,0,1:T(8,128)S(1)} %reverse_select_fusion.15, f32[137,4,128]{2,0,1:T(8,128)S(1)} %convolution_bitcast_fusion.15, f32[137,4,128]{2,1,0:T(4,128)S(1)} %copy-done.4, f32[137,137]{1,0:T(8,128)S(1)} %copy-done, f32[]{:T(128)} %bitcast.9, ...), kind=kOutput, calls=%fused_computation.29 | convolution fusion | flops 116719616 | bytes 1477976 | tf_op jit(solution)/shard_map/kl,lji->kji/dot_general | solution.py:100
  37.6 5.3 %collective-permute-start.6 = (f32[137,4,128]{2,0,1:T(8,128)S(1)}, f32[137,4,128]{2,0,1:T(8,128)}, u32[]{:S(2)}, u32[]{:S(2)}) collective-permute-start(f32[137,4,128]{2,0,1:T(8,128)S(1)} %convolution_bitcast_fusion.13), channel_id=1, source_target_pairs={{0,1},{1,2},{2,3},{4,5},{5,6},{6,7},{8,9},{9,10},{10,11},{12,13},{... | collective-permute-start | bytes 841736 | tf_op jit(solution)/shard_map/ppermute | solution.py:16
  42.9 1.3 collective-permute-start.7
  44.2 7.4 %collective-permute-done.5 = f32[137,8,128]{2,1,0:T(8,128)S(1)} collective-permute-done((f32[137,8,128]{2,1,0:T(8,128)S(1)}, f32[137,8,128]{2,1,0:T(8,128)S(1)}, u32[]{:S(2)}, u32[]{:S(2)}) %collective-permute-start.5) | collective-permute-done | bytes 561184 | tf_op jit(solution)/shard_map/ppermute | solution.py:25
  53.5 3.5 fusion.139
  57.2 2.6 collective-permute-start.9
  59.8 7.0 %collective-permute-done.8 = f32[137,4,32]{2,0,1:T(8,128)S(1)} collective-permute-done((f32[137,4,32]{2,0,1:T(8,128)S(1)}, f32[137,4,32]{2,0,1:T(8,128)S(1)}, u32[]{:S(2)}, u32[]{:S(2)}) %collective-permute-start.8) | collective-permute-done | bytes 70176 | tf_op jit(solution)/shard_map/ppermute | solution.py:16
  67.9 2.5 collective-permute-start.11
  70.5 7.3 %collective-permute-done.10 = f32[137,4,32]{2,0,1:T(8,128)S(1)} collective-permute-done((f32[137,4,32]{2,0,1:T(8,128)S(1)}, f32[137,4,32]{2,0,1:T(8,128)S(1)}, u32[]{:S(2)}, u32[]{:S(2)}) %collective-permute-start.10) | collective-permute-done | bytes 70176 | tf_op jit(solution)/shard_map/ppermute | solution.py:16
  79.5 5.6 %collective-permute-start.13 = (f32[137,4,128]{2,0,1:T(8,128)S(1)}, f32[137,4,128]{2,0,1:T(8,128)}, u32[]{:S(2)}, u32[]{:S(2)}) collective-permute-start(f32[137,4,128]{2,0,1:T(8,128)S(1)} %convolution_bitcast_fusion.11), channel_id=1, source_target_pairs={{0,1},{1,2},{2,3},{4,5},{5,6},{6,7},{8,9},{9,10},{10,11},{12,13},{... | collective-permute-start | bytes 841736 | tf_op jit(solution)/shard_map/ppermute | solution.py:16
  85.1 1.5 collective-permute-start.14
  86.6 6.5 %collective-permute-done.12 = f32[137,8,128]{2,1,0:T(8,128)S(1)} collective-permute-done((f32[137,8,128]{2,1,0:T(8,128)S(1)}, f32[137,8,128]{2,1,0:T(8,128)S(1)}, u32[]{:S(2)}, u32[]{:S(2)}) %collective-permute-start.12) | collective-permute-done | bytes 561184 | tf_op jit(solution)/shard_map/ppermute | solution.py:25
  96.4 3.9 %fusion.4 = f32[137,4,128]{2,0,1:T(8,128)S(1)} fusion(f32[137,4,128]{2,0,1:T(8,128)S(1)} %reverse_select_fusion.10, f32[137,4,128]{2,0,1:T(8,128)S(1)} %reverse_select_fusion.11, f32[137,4,128]{2,0,1:T(8,128)S(1)} %convolution_bitcast_fusion.11, f32[137,4,128]{2,1,0:T(4,128)S(1)} %copy-done.5, f32[137,137]{1,0:T(8,128)S(1)} %copy-done, f32[]{:T(128)} %bitcast.9, ...), kind=kOutput, calls=%fused_computation.24 | convolution fusion | flops 116719616 | bytes 1477976 | tf_op jit(solution)/shard_map/kl,lji->kji/dot_general | solution.py:100
  101.7 6.7 %collective-permute-start.16 = (f32[137,4,128]{2,0,1:T(8,128)S(1)}, f32[137,4,128]{2,0,1:T(8,128)}, u32[]{:S(2)}, u32[]{:S(2)}) collective-permute-start(f32[137,4,128]{2,0,1:T(8,128)S(1)} %convolution_bitcast_fusion.9), channel_id=1, source_target_pairs={{0,1},{1,2},{2,3},{4,5},{5,6},{6,7},{8,9},{9,10},{10,11},{12,13},{... | collective-permute-start | bytes 841736 | tf_op jit(solution)/shard_map/ppermute | solution.py:16
  109.7 4.6 %collective-permute-done.15 = f32[137,8,128]{2,1,0:T(8,128)S(1)} collective-permute-done((f32[137,8,128]{2,1,0:T(8,128)S(1)}, f32[137,8,128]{2,1,0:T(8,128)S(1)}, u32[]{:S(2)}, u32[]{:S(2)}) %collective-permute-start.15) | collective-permute-done | bytes 561184 | tf_op jit(solution)/shard_map/ppermute | solution.py:25
  116.2 1.8 collective-permute-done.17
  118.9 3.4 fusion.111
  122.6 2.6 collective-permute-start.19
  126.0 6.3 %collective-permute-done.18 = f32[137,4,32]{2,0,1:T(8,128)S(1)} collective-permute-done((f32[137,4,32]{2,0,1:T(8,128)S(1)}, f32[137,4,32]{2,0,1:T(8,128)S(1)}, u32[]{:S(2)}, u32[]{:S(2)}) %collective-permute-start.18) | collective-permute-done | bytes 70176 | tf_op jit(solution)/shard_map/ppermute | solution.py:16
  132.3 1.5 multiply_reduce_fusion.6
  133.8 40.9 %all-reduce.1 = (f32[]{:T(128)}, f32[]{:T(128)}, f32[]{:T(128)}, f32[]{:T(128)}) all-reduce(f32[]{:T(128)} %get-tuple-element.18, f32[]{:T(128)} %get-tuple-element.19, f32[]{:T(128)} %multiply_reduce_fusion.7, f32[]{:T(128)} %get-tuple-element.17), channel_id=1, replica_groups=mesh['lon'=8,'lat'=4] {'lon','lat'}, use_global_device_ids=true, to_apply=%region_9.11 | all-reduce | flops 4 | bytes 32 | tf_op jit(solution)/shard_map/psum | solution.py:113
  182.6 2.6 collective-permute-start.21
  185.3 4.5 %collective-permute-done.20 = f32[137,4,32]{2,0,1:T(8,128)S(1)} collective-permute-done((f32[137,4,32]{2,0,1:T(8,128)S(1)}, f32[137,4,32]{2,0,1:T(8,128)S(1)}, u32[]{:S(2)}, u32[]{:S(2)}) %collective-permute-start.20) | collective-permute-done | bytes 70176 | tf_op jit(solution)/shard_map/ppermute | solution.py:16
  189.8 2.0 collective-permute-done.21
  191.7 1.5 convolution_bitcast_fusion.7
  194.5 3.1 collective-permute-start.22
  197.6 2.6 collective-permute-start.23
  201.5 9.7 %collective-permute-done.22 = f32[137,8,128]{2,1,0:T(8,128)S(1)} collective-permute-done((f32[137,8,128]{2,1,0:T(8,128)S(1)}, f32[137,8,128]{2,1,0:T(8,128)S(1)}, u32[]{:S(2)}, u32[]{:S(2)}) %collective-permute-start.22) | collective-permute-done | bytes 561184 | tf_op jit(solution)/shard_map/ppermute | solution.py:25
  214.1 5.3 %fusion.3 = f32[137,4,128]{2,0,1:T(8,128)S(1)} fusion(f32[137,4,128]{2,0,1:T(8,128)S(1)} %reverse_select_fusion.6, f32[137,4,128]{2,0,1:T(8,128)S(1)} %reverse_select_fusion.7, f32[137,4,128]{2,0,1:T(8,128)} %convolution_bitcast_fusion.7, f32[137,4,128]{2,1,0:T(4,128)S(1)} %copy-done.6, f32[137,137]{1,0:T(8,128)S(1)} %copy-done, f32[]{:T(128)} %bitcast.9, ...), kind=kOutput, calls=%fused_computation.19 | convolution fusion | flops 116719616 | bytes 1477976 | tf_op jit(solution)/shard_map/kl,lji->kji/dot_general | solution.py:100
  220.6 3.5 collective-permute-start.26
  224.2 1.5 collective-permute-start.27
  225.7 9.4 %collective-permute-done.25 = f32[137,8,128]{2,1,0:T(8,128)S(1)} collective-permute-done((f32[137,8,128]{2,1,0:T(8,128)S(1)}, f32[137,8,128]{2,1,0:T(8,128)S(1)}, u32[]{:S(2)}, u32[]{:S(2)}) %collective-permute-start.25) | collective-permute-done | bytes 561184 | tf_op jit(solution)/shard_map/ppermute | solution.py:25
  235.6 1.7 gather_fusion.5
  237.3 1.6 copy.216
  240.1 3.4 fusion.83
  243.7 2.6 collective-permute-start.29
  246.3 7.2 %collective-permute-done.28 = f32[137,4,32]{2,0,1:T(8,128)S(1)} collective-permute-done((f32[137,4,32]{2,0,1:T(8,128)S(1)}, f32[137,4,32]{2,0,1:T(8,128)S(1)}, u32[]{:S(2)}, u32[]{:S(2)}) %collective-permute-start.28) | collective-permute-done | bytes 70176 | tf_op jit(solution)/shard_map/ppermute | solution.py:16
  254.6 2.6 collective-permute-start.31
  257.2 7.1 %collective-permute-done.30 = f32[137,4,32]{2,0,1:T(8,128)S(1)} collective-permute-done((f32[137,4,32]{2,0,1:T(8,128)S(1)}, f32[137,4,32]{2,0,1:T(8,128)S(1)}, u32[]{:S(2)}, u32[]{:S(2)}) %collective-permute-start.30) | collective-permute-done | bytes 70176 | tf_op jit(solution)/shard_map/ppermute | solution.py:16
  265.5 4.5 %collective-permute-start.33 = (f32[137,4,128]{2,0,1:T(8,128)S(1)}, f32[137,4,128]{2,0,1:T(8,128)}, u32[]{:S(2)}, u32[]{:S(2)}) collective-permute-start(f32[137,4,128]{2,0,1:T(8,128)S(1)} %convolution_bitcast_fusion.3), channel_id=1, source_target_pairs={{0,1},{1,2},{2,3},{4,5},{5,6},{6,7},{8,9},{9,10},{10,11},{12,13},{... | collective-permute-start | bytes 841736 | tf_op jit(solution)/shard_map/ppermute | solution.py:16
  271.2 7.6 %collective-permute-done.32 = f32[137,8,128]{2,1,0:T(8,128)} collective-permute-done((f32[137,8,128]{2,1,0:T(8,128)S(1)}, f32[137,8,128]{2,1,0:T(8,128)}, u32[]{:S(2)}, u32[]{:S(2)}) %collective-permute-start.32) | collective-permute-done | bytes 561184 | tf_op jit(solution)/shard_map/ppermute | solution.py:25
  278.9 1.6 copy.220
  280.4 1.7 gather_fusion.6
  282.2 1.6 copy.221
  284.8 3.9 %fusion.2 = f32[137,4,128]{2,0,1:T(8,128)S(1)} fusion(f32[137,4,128]{2,0,1:T(8,128)S(1)} %reverse_select_fusion.2, f32[137,4,128]{2,0,1:T(8,128)S(1)} %reverse_select_fusion.3, f32[137,4,128]{2,0,1:T(8,128)S(1)} %convolution_bitcast_fusion.3, f32[137,4,128]{2,1,0:T(4,128)S(1)} %copy-done.7, f32[137,137]{1,0:T(8,128)S(1)} %copy-done, f32[]{:T(128)} %bitcast.9, ...), kind=kOutput, calls=%fused_computation.14 | convolution fusion | flops 116719616 | bytes 1477976 | tf_op jit(solution)/shard_map/kl,lji->kji/dot_general | solution.py:100
  289.5 1.4 collective-permute-start.35
  290.9 4.9 %collective-permute-start.36 = (f32[137,4,128]{2,0,1:T(8,128)S(1)}, f32[137,4,128]{2,0,1:T(8,128)}, u32[]{:S(2)}, u32[]{:S(2)}) collective-permute-start(f32[137,4,128]{2,0,1:T(8,128)S(1)} %convolution_bitcast_fusion.1), channel_id=1, source_target_pairs={{0,1},{1,2},{2,3},{4,5},{5,6},{6,7},{8,9},{9,10},{10,11},{12,13},{... | collective-permute-start | bytes 841736 | tf_op jit(solution)/shard_map/ppermute | solution.py:16
  297.1 6.0 %collective-permute-done.35 = f32[137,8,128]{2,1,0:T(8,128)} collective-permute-done((f32[137,8,128]{2,1,0:T(8,128)S(1)}, f32[137,8,128]{2,1,0:T(8,128)}, u32[]{:S(2)}, u32[]{:S(2)}) %collective-permute-start.35) | collective-permute-done | bytes 561184 | tf_op jit(solution)/shard_map/ppermute | solution.py:25
  303.1 1.6 copy.225
  304.6 1.7 gather_fusion.7
  306.4 1.6 copy.226
  308.2 3.4 fusion.55
  311.8 2.6 collective-permute-start.39
  314.4 5.4 %collective-permute-done.38 = f32[137,4,32]{2,0,1:T(8,128)S(1)} collective-permute-done((f32[137,4,32]{2,0,1:T(8,128)S(1)}, f32[137,4,32]{2,0,1:T(8,128)S(1)}, u32[]{:S(2)}, u32[]{:S(2)}) %collective-permute-start.38) | collective-permute-done | bytes 70176 | tf_op jit(solution)/shard_map/ppermute | solution.py:16
  320.3 1.5 multiply_reduce_fusion.3
  321.8 42.7 %all-reduce = (f32[]{:T(128)}, f32[]{:T(128)}, f32[]{:T(128)}, f32[]{:T(128)}) all-reduce(f32[]{:T(128)} %get-tuple-element.14, f32[]{:T(128)} %get-tuple-element.16, f32[]{:T(128)} %get-tuple-element.15, f32[]{:T(128)} %get-tuple-element.13), channel_id=1, replica_groups=mesh['lon'=8,'lat'=4] {'lon','lat'}, use_global_device_ids=true, to_apply=%region_17.19 | all-reduce | flops 4 | bytes 32 | tf_op jit(solution)/shard_map/psum | solution.py:113
  (157 shorter events, 42.2 us)
Async XLA Ops:
  0.6 31.1 %copy-start = (f32[137,137]{1,0:T(8,128)S(1)}, f32[137,137]{1,0:T(8,128)}, u32[]{:S(2)}) copy-start(f32[137,137]{1,0:T(8,128)} %param.15) | copy-start | bytes 225232
  0.6 4.6 %copy-start.3 = (s32[4]{0:T(128)S(1)}, s32[4]{0:T(128)}, u32[]{:S(2)}) copy-start(s32[4]{0:T(128)} %param.11) | copy-start | bytes 52
  0.7 4.6 %copy-start.2 = (f32[4,33]{1,0:T(4,128)S(1)}, f32[4,33]{1,0:T(4,128)}, u32[]{:S(2)}) copy-start(f32[4,33]{1,0:T(4,128)} %param.12) | copy-start | bytes 1588
  0.7 5.2 %copy-start.9 = (f32[5]{0:T(128)S(1)}, f32[5]{0:T(128)}, u32[]{:S(2)}) copy-start(f32[5]{0:T(128)} %param.14) | copy-start | bytes 64
  1.8 8.3 %collective-permute-start = (f32[137,4,32]{2,0,1:T(8,128)S(1)}, f32[137,4,32]{2,0,1:T(8,128)S(1)}, u32[]{:S(2)}, u32[]{:S(2)}) collective-permute-start(f32[137,4,32]{2,0,1:T(8,128)S(1)} %get-tuple-element.62), channel_id=1, source_target_pairs={{0,4},{4,8},{8,12},{12,16},{16,20},{20,24},{24,28},{28,0},{1,5},{5... | collective-permute-start | bytes 210440 | tf_op jit(solution)/shard_map/ppermute | solution.py:16
  2.3 9.3 %collective-permute-start.1 = (f32[137,4,32]{2,0,1:T(8,128)S(1)}, f32[137,4,32]{2,0,1:T(8,128)S(1)}, u32[]{:S(2)}, u32[]{:S(2)}) collective-permute-start(f32[137,4,32]{2,0,1:T(8,128)S(1)} %get-tuple-element.63), channel_id=1, source_target_pairs={{4,0},{8,4},{12,8},{16,12},{20,16},{24,20},{28,24},{0,28},{5,1},{9... | collective-permute-start | bytes 210440 | tf_op jit(solution)/shard_map/ppermute | solution.py:19
  12.5 2.9 copy-start.8
  12.7 16.0 %collective-permute-start.2 = (f32[137,8,128]{2,1,0:T(8,128)S(1)}, f32[137,8,128]{2,1,0:T(8,128)S(1)}, u32[]{:S(2)}, u32[]{:S(2)}) collective-permute-start(f32[137,8,128]{2,1,0:T(8,128)S(1)} %copy.185), channel_id=1, source_target_pairs={{0,16},{4,20},{8,24},{12,28},{16,0},{20,4},{24,8},{28,12},{1,17},{... | collective-permute-start | bytes 1683464 | tf_op jit(solution)/shard_map/ppermute | solution.py:25
  16.1 14.5 %collective-permute-start.3 = (f32[137,4,128]{2,0,1:T(8,128)S(1)}, f32[137,4,128]{2,0,1:T(8,128)}, u32[]{:S(2)}, u32[]{:S(2)}) collective-permute-start(f32[137,4,128]{2,0,1:T(8,128)S(1)} %convolution_bitcast_fusion.15), channel_id=1, source_target_pairs={{0,1},{1,2},{2,3},{4,5},{5,6},{6,7},{8,9},{9,10},{10,11},{12,13},{... | collective-permute-start | bytes 841736 | tf_op jit(solution)/shard_map/ppermute | solution.py:16
  20.3 10.4 %collective-permute-start.4 = (f32[137,4,128]{2,0,1:T(8,128)S(1)}, f32[137,4,128]{2,0,1:T(8,128)}, u32[]{:S(2)}, u32[]{:S(2)}) collective-permute-start(f32[137,4,128]{2,0,1:T(8,128)S(1)} %convolution_bitcast_fusion.15), channel_id=1, source_target_pairs={{1,0},{2,1},{3,2},{5,4},{6,5},{7,6},{9,8},{10,9},{11,10},{13,12},{... | collective-permute-start | bytes 841736 | tf_op jit(solution)/shard_map/ppermute | solution.py:19
  30.6 1.1 copy-start.4
  36.4 15.1 %collective-permute-start.5 = (f32[137,8,128]{2,1,0:T(8,128)S(1)}, f32[137,8,128]{2,1,0:T(8,128)S(1)}, u32[]{:S(2)}, u32[]{:S(2)}) collective-permute-start(f32[137,8,128]{2,1,0:T(8,128)S(1)} %copy.190), channel_id=1, source_target_pairs={{0,16},{4,20},{8,24},{12,28},{16,0},{20,4},{24,8},{28,12},{1,17},{... | collective-permute-start | bytes 1683464 | tf_op jit(solution)/shard_map/ppermute | solution.py:25
  37.6 15.8 %collective-permute-start.6 = (f32[137,4,128]{2,0,1:T(8,128)S(1)}, f32[137,4,128]{2,0,1:T(8,128)}, u32[]{:S(2)}, u32[]{:S(2)}) collective-permute-start(f32[137,4,128]{2,0,1:T(8,128)S(1)} %convolution_bitcast_fusion.13), channel_id=1, source_target_pairs={{0,1},{1,2},{2,3},{4,5},{5,6},{6,7},{8,9},{9,10},{10,11},{12,13},{... | collective-permute-start | bytes 841736 | tf_op jit(solution)/shard_map/ppermute | solution.py:16
  42.9 10.6 %collective-permute-start.7 = (f32[137,4,128]{2,0,1:T(8,128)S(1)}, f32[137,4,128]{2,0,1:T(8,128)S(1)}, u32[]{:S(2)}, u32[]{:S(2)}) collective-permute-start(f32[137,4,128]{2,0,1:T(8,128)S(1)} %convolution_bitcast_fusion.13), channel_id=1, source_target_pairs={{1,0},{2,1},{3,2},{5,4},{6,5},{7,6},{9,8},{10,9},{11,10},{13,12},{... | collective-permute-start | bytes 841736 | tf_op jit(solution)/shard_map/ppermute | solution.py:19
  53.5 13.3 %copy-start.1 = (f32[137,4,128]{2,1,0:T(4,128)S(1)}, f32[137,4,128]{2,1,0:T(4,128)}, u32[]{:S(2)}) copy-start(f32[137,4,128]{2,1,0:T(4,128)} %param.9) | copy-start | bytes 841732
  57.1 9.7 %collective-permute-start.8 = (f32[137,4,32]{2,0,1:T(8,128)S(1)}, f32[137,4,32]{2,0,1:T(8,128)S(1)}, u32[]{:S(2)}, u32[]{:S(2)}) collective-permute-start(f32[137,4,32]{2,0,1:T(8,128)S(1)} %get-tuple-element.60), channel_id=1, source_target_pairs={{0,4},{4,8},{8,12},{12,16},{16,20},{20,24},{24,28},{28,0},{1,5},{5... | collective-permute-start | bytes 210440 | tf_op jit(solution)/shard_map/ppermute | solution.py:16
  57.2 9.6 %collective-permute-start.9 = (f32[137,4,32]{2,0,1:T(8,128)S(1)}, f32[137,4,32]{2,0,1:T(8,128)S(1)}, u32[]{:S(2)}, u32[]{:S(2)}) collective-permute-start(f32[137,4,32]{2,0,1:T(8,128)S(1)} %get-tuple-element.61), channel_id=1, source_target_pairs={{4,0},{8,4},{12,8},{16,12},{20,16},{24,20},{28,24},{0,28},{5,1},{9... | collective-permute-start | bytes 210440 | tf_op jit(solution)/shard_map/ppermute | solution.py:19
  67.8 10.0 %collective-permute-start.10 = (f32[137,4,32]{2,0,1:T(8,128)S(1)}, f32[137,4,32]{2,0,1:T(8,128)S(1)}, u32[]{:S(2)}, u32[]{:S(2)}) collective-permute-start(f32[137,4,32]{2,0,1:T(8,128)S(1)} %get-tuple-element.58), channel_id=1, source_target_pairs={{0,4},{4,8},{8,12},{12,16},{16,20},{20,24},{24,28},{28,0},{1,5},{5... | collective-permute-start | bytes 210440 | tf_op jit(solution)/shard_map/ppermute | solution.py:16
  67.9 9.9 %collective-permute-start.11 = (f32[137,4,32]{2,0,1:T(8,128)S(1)}, f32[137,4,32]{2,0,1:T(8,128)S(1)}, u32[]{:S(2)}, u32[]{:S(2)}) collective-permute-start(f32[137,4,32]{2,0,1:T(8,128)S(1)} %get-tuple-element.59), channel_id=1, source_target_pairs={{4,0},{8,4},{12,8},{16,12},{20,16},{24,20},{28,24},{0,28},{5,1},{9... | collective-permute-start | bytes 210440 | tf_op jit(solution)/shard_map/ppermute | solution.py:19
  78.9 14.2 %collective-permute-start.12 = (f32[137,8,128]{2,1,0:T(8,128)S(1)}, f32[137,8,128]{2,1,0:T(8,128)S(1)}, u32[]{:S(2)}, u32[]{:S(2)}) collective-permute-start(f32[137,8,128]{2,1,0:T(8,128)S(1)} %copy.196), channel_id=1, source_target_pairs={{0,16},{4,20},{8,24},{12,28},{16,0},{20,4},{24,8},{28,12},{1,17},{... | collective-permute-start | bytes 1683464 | tf_op jit(solution)/shard_map/ppermute | solution.py:25
  79.5 15.4 %collective-permute-start.13 = (f32[137,4,128]{2,0,1:T(8,128)S(1)}, f32[137,4,128]{2,0,1:T(8,128)}, u32[]{:S(2)}, u32[]{:S(2)}) collective-permute-start(f32[137,4,128]{2,0,1:T(8,128)S(1)} %convolution_bitcast_fusion.11), channel_id=1, source_target_pairs={{0,1},{1,2},{2,3},{4,5},{5,6},{6,7},{8,9},{9,10},{10,11},{12,13},{... | collective-permute-start | bytes 841736 | tf_op jit(solution)/shard_map/ppermute | solution.py:16
  85.1 10.3 %collective-permute-start.14 = (f32[137,4,128]{2,0,1:T(8,128)S(1)}, f32[137,4,128]{2,0,1:T(8,128)}, u32[]{:S(2)}, u32[]{:S(2)}) collective-permute-start(f32[137,4,128]{2,0,1:T(8,128)S(1)} %convolution_bitcast_fusion.11), channel_id=1, source_target_pairs={{1,0},{2,1},{3,2},{5,4},{6,5},{7,6},{9,8},{10,9},{11,10},{13,12},{... | collective-permute-start | bytes 841736 | tf_op jit(solution)/shard_map/ppermute | solution.py:19
  94.9 1.5 copy-start.5
  101.1 13.2 %collective-permute-start.15 = (f32[137,8,128]{2,1,0:T(8,128)S(1)}, f32[137,8,128]{2,1,0:T(8,128)S(1)}, u32[]{:S(2)}, u32[]{:S(2)}) collective-permute-start(f32[137,8,128]{2,1,0:T(8,128)S(1)} %copy.201), channel_id=1, source_target_pairs={{0,16},{4,20},{8,24},{12,28},{16,0},{20,4},{24,8},{28,12},{1,17},{... | collective-permute-start | bytes 1683464 | tf_op jit(solution)/shard_map/ppermute | solution.py:25
  101.7 14.4 %collective-permute-start.16 = (f32[137,4,128]{2,0,1:T(8,128)S(1)}, f32[137,4,128]{2,0,1:T(8,128)}, u32[]{:S(2)}, u32[]{:S(2)}) collective-permute-start(f32[137,4,128]{2,0,1:T(8,128)S(1)} %convolution_bitcast_fusion.9), channel_id=1, source_target_pairs={{0,1},{1,2},{2,3},{4,5},{5,6},{6,7},{8,9},{9,10},{10,11},{12,13},{... | collective-permute-start | bytes 841736 | tf_op jit(solution)/shard_map/ppermute | solution.py:16
  108.4 9.6 %collective-permute-start.17 = (f32[137,4,128]{2,0,1:T(8,128)S(1)}, f32[137,4,128]{2,0,1:T(8,128)}, u32[]{:S(2)}, u32[]{:S(2)}) collective-permute-start(f32[137,4,128]{2,0,1:T(8,128)S(1)} %convolution_bitcast_fusion.9), channel_id=1, source_target_pairs={{1,0},{2,1},{3,2},{5,4},{6,5},{7,6},{9,8},{10,9},{11,10},{13,12},{... | collective-permute-start | bytes 841736 | tf_op jit(solution)/shard_map/ppermute | solution.py:19
  122.5 9.8 %collective-permute-start.18 = (f32[137,4,32]{2,0,1:T(8,128)S(1)}, f32[137,4,32]{2,0,1:T(8,128)S(1)}, u32[]{:S(2)}, u32[]{:S(2)}) collective-permute-start(f32[137,4,32]{2,0,1:T(8,128)S(1)} %get-tuple-element.56), channel_id=1, source_target_pairs={{0,4},{4,8},{8,12},{12,16},{16,20},{20,24},{24,28},{28,0},{1,5},{5... | collective-permute-start | bytes 210440 | tf_op jit(solution)/shard_map/ppermute | solution.py:16
  122.6 9.7 %collective-permute-start.19 = (f32[137,4,32]{2,0,1:T(8,128)S(1)}, f32[137,4,32]{2,0,1:T(8,128)S(1)}, u32[]{:S(2)}, u32[]{:S(2)}) collective-permute-start(f32[137,4,32]{2,0,1:T(8,128)S(1)} %get-tuple-element.57), channel_id=1, source_target_pairs={{4,0},{8,4},{12,8},{16,12},{20,16},{24,20},{28,24},{0,28},{5,1},{9... | collective-permute-start | bytes 210440 | tf_op jit(solution)/shard_map/ppermute | solution.py:19
  182.6 7.2 %collective-permute-start.20 = (f32[137,4,32]{2,0,1:T(8,128)S(1)}, f32[137,4,32]{2,0,1:T(8,128)S(1)}, u32[]{:S(2)}, u32[]{:S(2)}) collective-permute-start(f32[137,4,32]{2,0,1:T(8,128)S(1)} %get-tuple-element.54), channel_id=1, source_target_pairs={{0,4},{4,8},{8,12},{12,16},{16,20},{20,24},{24,28},{28,0},{1,5},{5... | collective-permute-start | bytes 210440 | tf_op jit(solution)/shard_map/ppermute | solution.py:16
  182.6 9.1 %collective-permute-start.21 = (f32[137,4,32]{2,0,1:T(8,128)S(1)}, f32[137,4,32]{2,0,1:T(8,128)S(1)}, u32[]{:S(2)}, u32[]{:S(2)}) collective-permute-start(f32[137,4,32]{2,0,1:T(8,128)S(1)} %get-tuple-element.55), channel_id=1, source_target_pairs={{4,0},{8,4},{12,8},{16,12},{20,16},{24,20},{28,24},{0,28},{5,1},{9... | collective-permute-start | bytes 210440 | tf_op jit(solution)/shard_map/ppermute | solution.py:19
  194.5 16.6 %collective-permute-start.22 = (f32[137,8,128]{2,1,0:T(8,128)S(1)}, f32[137,8,128]{2,1,0:T(8,128)S(1)}, u32[]{:S(2)}, u32[]{:S(2)}) collective-permute-start(f32[137,8,128]{2,1,0:T(8,128)S(1)} %copy.209), channel_id=1, source_target_pairs={{0,16},{4,20},{8,24},{12,28},{16,0},{20,4},{24,8},{28,12},{1,17},{... | collective-permute-start | bytes 1683464 | tf_op jit(solution)/shard_map/ppermute | solution.py:25
  197.6 15.4 %collective-permute-start.23 = (f32[137,4,128]{2,0,1:T(8,128)}, f32[137,4,128]{2,0,1:T(8,128)}, u32[]{:S(2)}, u32[]{:S(2)}) collective-permute-start(f32[137,4,128]{2,0,1:T(8,128)} %convolution_bitcast_fusion.7), channel_id=1, source_target_pairs={{0,1},{1,2},{2,3},{4,5},{5,6},{6,7},{8,9},{9,10},{10,11},{12,13},{... | collective-permute-start | bytes 841736 | tf_op jit(solution)/shard_map/ppermute | solution.py:16
  200.2 12.9 %collective-permute-start.24 = (f32[137,4,128]{2,0,1:T(8,128)}, f32[137,4,128]{2,0,1:T(8,128)}, u32[]{:S(2)}, u32[]{:S(2)}) collective-permute-start(f32[137,4,128]{2,0,1:T(8,128)} %convolution_bitcast_fusion.7), channel_id=1, source_target_pairs={{1,0},{2,1},{3,2},{5,4},{6,5},{7,6},{9,8},{10,9},{11,10},{13,12},{... | collective-permute-start | bytes 841736 | tf_op jit(solution)/shard_map/ppermute | solution.py:19
  213.0 1.1 copy-start.6
  220.3 14.8 %collective-permute-start.25 = (f32[137,8,128]{2,1,0:T(8,128)S(1)}, f32[137,8,128]{2,1,0:T(8,128)S(1)}, u32[]{:S(2)}, u32[]{:S(2)}) collective-permute-start(f32[137,8,128]{2,1,0:T(8,128)S(1)} %copy.214), channel_id=1, source_target_pairs={{0,16},{4,20},{8,24},{12,28},{16,0},{20,4},{24,8},{28,12},{1,17},{... | collective-permute-start | bytes 1683464 | tf_op jit(solution)/shard_map/ppermute | solution.py:25
  220.6 18.4 %collective-permute-start.26 = (f32[137,4,128]{2,0,1:T(8,128)S(1)}, f32[137,4,128]{2,0,1:T(8,128)}, u32[]{:S(2)}, u32[]{:S(2)}) collective-permute-start(f32[137,4,128]{2,0,1:T(8,128)S(1)} %convolution_bitcast_fusion.5), channel_id=1, source_target_pairs={{0,1},{1,2},{2,3},{4,5},{5,6},{6,7},{8,9},{9,10},{10,11},{12,13},{... | collective-permute-start | bytes 841736 | tf_op jit(solution)/shard_map/ppermute | solution.py:16
  224.2 14.9 %collective-permute-start.27 = (f32[137,4,128]{2,0,1:T(8,128)S(1)}, f32[137,4,128]{2,0,1:T(8,128)}, u32[]{:S(2)}, u32[]{:S(2)}) collective-permute-start(f32[137,4,128]{2,0,1:T(8,128)S(1)} %convolution_bitcast_fusion.5), channel_id=1, source_target_pairs={{1,0},{2,1},{3,2},{5,4},{6,5},{7,6},{9,8},{10,9},{11,10},{13,12},{... | collective-permute-start | bytes 841736 | tf_op jit(solution)/shard_map/ppermute | solution.py:19
  243.6 9.9 %collective-permute-start.28 = (f32[137,4,32]{2,0,1:T(8,128)S(1)}, f32[137,4,32]{2,0,1:T(8,128)S(1)}, u32[]{:S(2)}, u32[]{:S(2)}) collective-permute-start(f32[137,4,32]{2,0,1:T(8,128)S(1)} %get-tuple-element.52), channel_id=1, source_target_pairs={{0,4},{4,8},{8,12},{12,16},{16,20},{20,24},{24,28},{28,0},{1,5},{5... | collective-permute-start | bytes 210440 | tf_op jit(solution)/shard_map/ppermute | solution.py:16
  243.7 9.8 %collective-permute-start.29 = (f32[137,4,32]{2,0,1:T(8,128)S(1)}, f32[137,4,32]{2,0,1:T(8,128)S(1)}, u32[]{:S(2)}, u32[]{:S(2)}) collective-permute-start(f32[137,4,32]{2,0,1:T(8,128)S(1)} %get-tuple-element.53), channel_id=1, source_target_pairs={{4,0},{8,4},{12,8},{16,12},{20,16},{24,20},{28,24},{0,28},{5,1},{9... | collective-permute-start | bytes 210440 | tf_op jit(solution)/shard_map/ppermute | solution.py:19
  254.5 9.8 %collective-permute-start.30 = (f32[137,4,32]{2,0,1:T(8,128)S(1)}, f32[137,4,32]{2,0,1:T(8,128)S(1)}, u32[]{:S(2)}, u32[]{:S(2)}) collective-permute-start(f32[137,4,32]{2,0,1:T(8,128)S(1)} %get-tuple-element.50), channel_id=1, source_target_pairs={{0,4},{4,8},{8,12},{12,16},{16,20},{20,24},{24,28},{28,0},{1,5},{5... | collective-permute-start | bytes 210440 | tf_op jit(solution)/shard_map/ppermute | solution.py:16
  254.6 9.7 %collective-permute-start.31 = (f32[137,4,32]{2,0,1:T(8,128)S(1)}, f32[137,4,32]{2,0,1:T(8,128)S(1)}, u32[]{:S(2)}, u32[]{:S(2)}) collective-permute-start(f32[137,4,32]{2,0,1:T(8,128)S(1)} %get-tuple-element.51), channel_id=1, source_target_pairs={{4,0},{8,4},{12,8},{16,12},{20,16},{24,20},{28,24},{0,28},{5,1},{9... | collective-permute-start | bytes 210440 | tf_op jit(solution)/shard_map/ppermute | solution.py:19
  265.4 13.5 %collective-permute-start.32 = (f32[137,8,128]{2,1,0:T(8,128)S(1)}, f32[137,8,128]{2,1,0:T(8,128)}, u32[]{:S(2)}, u32[]{:S(2)}) collective-permute-start(f32[137,8,128]{2,1,0:T(8,128)S(1)} %copy.219), channel_id=1, source_target_pairs={{0,16},{4,20},{8,24},{12,28},{16,0},{20,4},{24,8},{28,12},{1,17},{... | collective-permute-start | bytes 1683464 | tf_op jit(solution)/shard_map/ppermute | solution.py:25
  265.5 18.4 %collective-permute-start.33 = (f32[137,4,128]{2,0,1:T(8,128)S(1)}, f32[137,4,128]{2,0,1:T(8,128)}, u32[]{:S(2)}, u32[]{:S(2)}) collective-permute-start(f32[137,4,128]{2,0,1:T(8,128)S(1)} %convolution_bitcast_fusion.3), channel_id=1, source_target_pairs={{0,1},{1,2},{2,3},{4,5},{5,6},{6,7},{8,9},{9,10},{10,11},{12,13},{... | collective-permute-start | bytes 841736 | tf_op jit(solution)/shard_map/ppermute | solution.py:16
  269.9 14.0 %collective-permute-start.34 = (f32[137,4,128]{2,0,1:T(8,128)S(1)}, f32[137,4,128]{2,0,1:T(8,128)S(1)}, u32[]{:S(2)}, u32[]{:S(2)}) collective-permute-start(f32[137,4,128]{2,0,1:T(8,128)S(1)} %convolution_bitcast_fusion.3), channel_id=1, source_target_pairs={{1,0},{2,1},{3,2},{5,4},{6,5},{7,6},{9,8},{10,9},{11,10},{13,12},{... | collective-permute-start | bytes 841736 | tf_op jit(solution)/shard_map/ppermute | solution.py:19
  283.9 1.0 copy-start.7
  289.5 13.5 %collective-permute-start.35 = (f32[137,8,128]{2,1,0:T(8,128)S(1)}, f32[137,8,128]{2,1,0:T(8,128)}, u32[]{:S(2)}, u32[]{:S(2)}) collective-permute-start(f32[137,8,128]{2,1,0:T(8,128)S(1)} %copy.224), channel_id=1, source_target_pairs={{0,16},{4,20},{8,24},{12,28},{16,0},{20,4},{24,8},{28,12},{1,17},{... | collective-permute-start | bytes 1683464 | tf_op jit(solution)/shard_map/ppermute | solution.py:25
  290.9 17.2 %collective-permute-start.36 = (f32[137,4,128]{2,0,1:T(8,128)S(1)}, f32[137,4,128]{2,0,1:T(8,128)}, u32[]{:S(2)}, u32[]{:S(2)}) collective-permute-start(f32[137,4,128]{2,0,1:T(8,128)S(1)} %convolution_bitcast_fusion.1), channel_id=1, source_target_pairs={{0,1},{1,2},{2,3},{4,5},{5,6},{6,7},{8,9},{9,10},{10,11},{12,13},{... | collective-permute-start | bytes 841736 | tf_op jit(solution)/shard_map/ppermute | solution.py:16
  295.8 12.3 %collective-permute-start.37 = (f32[137,4,128]{2,0,1:T(8,128)S(1)}, f32[137,4,128]{2,0,1:T(8,128)S(1)}, u32[]{:S(2)}, u32[]{:S(2)}) collective-permute-start(f32[137,4,128]{2,0,1:T(8,128)S(1)} %convolution_bitcast_fusion.1), channel_id=1, source_target_pairs={{1,0},{2,1},{3,2},{5,4},{6,5},{7,6},{9,8},{10,9},{11,10},{13,12},{... | collective-permute-start | bytes 841736 | tf_op jit(solution)/shard_map/ppermute | solution.py:19
  311.7 8.1 %collective-permute-start.38 = (f32[137,4,32]{2,0,1:T(8,128)S(1)}, f32[137,4,32]{2,0,1:T(8,128)S(1)}, u32[]{:S(2)}, u32[]{:S(2)}) collective-permute-start(f32[137,4,32]{2,0,1:T(8,128)S(1)} %get-tuple-element.48), channel_id=1, source_target_pairs={{0,4},{4,8},{8,12},{12,16},{16,20},{20,24},{24,28},{28,0},{1,5},{5... | collective-permute-start | bytes 210440 | tf_op jit(solution)/shard_map/ppermute | solution.py:16
  311.8 8.5 %collective-permute-start.39 = (f32[137,4,32]{2,0,1:T(8,128)S(1)}, f32[137,4,32]{2,0,1:T(8,128)S(1)}, u32[]{:S(2)}, u32[]{:S(2)}) collective-permute-start(f32[137,4,32]{2,0,1:T(8,128)S(1)} %get-tuple-element.49), channel_id=1, source_target_pairs={{4,0},{8,4},{12,8},{16,12},{20,16},{24,20},{28,24},{0,28},{5,1},{9... | collective-permute-start | bytes 210440 | tf_op jit(solution)/shard_map/ppermute | solution.py:19
where the time goes:
time: 376 us; the launch traced here: 374 us
  waiting for transfers between devices  111 us (30%)
  blocking collectives  83.7 us (22%)
  starting transfers between devices  80.1 us (21%)
  local copies, waits for them, and re-layouts  29.5 us (8%)
  matrix products  29.1 us (8%)
  other arithmetic  23 us (6%)
  between operations  18 us (5%)
    psum x2, blocking collectives, per_device(): lax.psum((jnp.sum(residual * residual), jnp.sum(residual * first), jnp.su...  83.7 us
    ppermute x8, waiting for transfers between devices, from_partner(): lax.ppermute(value, axis, [(i, i ^ 1 << distance) for i in range(lax.axis...  58.4 us
    ppermute x16, waiting for transfers between devices, extended_2(): lax.ppermute(lax.slice_in_dim(block, block.shape[dim] - width, None, axis...  46.3 us
    ppermute x16, starting transfers between devices, extended_2(): lax.ppermute(lax.slice_in_dim(block, block.shape[dim] - width, None, axis...  38.2 us
    ppermute x16, starting transfers between devices, extended_2(): lax.ppermute(lax.slice_in_dim(block, 0, width, axis=dim), axis, backward)  31.9 us
    dot_general x4, matrix products, hessian(): jnp.einsum('kl,lji->kji', vertical_map, forward, precision=lax.Precision....  16.8 us
    gather x16, local copies, waits for them, and re-layouts, merid_apply(): mirrored = jnp.take(polar, mirror_local, axis=2)  16 us
    add x4, other arithmetic, merid_apply(): result = result + weights[offset] * (upper + lower)  13.7 us
  transfers between devices with their start and end apart: 40, of which 21 were waited for; matrix products, arithmetic and copies ran while one was open for 7% of the time, Pallas kernels for 0%

commit v1 on v0

--- a/solution.py
+++ b/solution.py
@@ -110,9 +110,16 @@
     residual = gradient
     for outer in range(OUTER):
         first = hessian(residual)
-        sum_rr, sum_rf, sum_ff = lax.psum(
-            (jnp.sum(residual * residual), jnp.sum(residual * first), jnp.sum(first * first)),
-            ("lon", "lat"),
+
+        def part_stops_all(sheet):
+            a_name = "lon"
+            comm_axis = "lat"
+            for to_i in (comm_axis, a_name):
+                sheet = lax.psum(sheet, to_i)
+            return sheet
+
+        sum_rr, sum_rf, sum_ff = part_stops_all(
+            (jnp.sum(residual * residual), jnp.sum(residual * first), jnp.sum(first * first))
         )
         second = hessian(first)
         sum_fs = lax.psum(jnp.sum(first * second), ("lon", "lat"))

time: 376 us -> 419 us (1.11)
  blocking collectives: 83.7 us -> 126 us
    psum x2 -> x6, blocking collectives: 83.7 us -> 126 us  [the longest x2 76.8 us: per_device(): sum_fs = lax.psum(jnp.sum(first * second), ('lon', 'lat'))]
  transfers between devices with their start and end apart: 40 -> 40, of which waited for: 21 -> 20; matrix products, arithmetic and copies ran while one was open for 7% -> 7% of each run, Pallas kernels for 0% -> 0%
where the time goes in v1:
time: 419 us; the launch traced here: 417 us
  blocking collectives  126 us (30%)
  waiting for transfers between devices  109 us (26%)
  starting transfers between devices  83.5 us (20%)
  local copies, waits for them, and re-layouts  30.4 us (7%)
  matrix products  28.3 us (7%)
  other arithmetic  21.3 us (5%)
  between operations  18.1 us (4%)
    psum x2, blocking collectives, per_device(): sum_fs = lax.psum(jnp.sum(first * second), ('lon', 'lat'))  76.8 us
    ppermute x8, waiting for transfers between devices, from_partner(): lax.ppermute(value, axis, [(i, i ^ 1 << distance) for i in range(lax.axis...  54.9 us
    psum x4, blocking collectives, part_stops_all(): sheet = lax.psum(sheet, to_i)  49.6 us
    ppermute x16, waiting for transfers between devices, extended_2(): lax.ppermute(lax.slice_in_dim(block, block.shape[dim] - width, None, axis...  47.7 us
    ppermute x16, starting transfers between devices, extended_2(): lax.ppermute(lax.slice_in_dim(block, block.shape[dim] - width, None, axis...  41.4 us
    ppermute x16, starting transfers between devices, extended_2(): lax.ppermute(lax.slice_in_dim(block, 0, width, axis=dim), axis, backward)  32 us
    dot_general x4, matrix products, hessian(): jnp.einsum('kl,lji->kji', vertical_map, forward, precision=lax.Precision....  16 us
    gather x16, local copies, waits for them, and re-layouts, merid_apply(): mirrored = jnp.take(polar, mirror_local, axis=2)  16 us
  transfers between devices with their start and end apart: 40, of which 20 were waited for; matrix products, arithmetic and copies ran while one was open for 7% of the time, Pallas kernels for 0%

profile of v1, /device:TPU:0, one launch (start us, length us, event | category | flops | bytes accessed | tf_op | source)
XLA Modules:
  0.0 416.6 jit_solution(2894125785209538530)
XLA Ops:
  2.3 2.9 collective-permute-start.1
  8.6 1.5 collective-permute-done
  10.1 1.5 collective-permute-done.1
  12.7 2.7 collective-permute-start.2
  16.1 3.5 collective-permute-start.3
  20.9 7.8 %collective-permute-done.2 = f32[137,8,128]{2,1,0:T(8,128)S(1)} collective-permute-done((f32[137,8,128]{2,1,0:T(8,128)S(1)}, f32[137,8,128]{2,1,0:T(8,128)S(1)}, u32[]{:S(2)}, u32[]{:S(2)}) %collective-permute-start.2) | collective-permute-done | bytes 561184 | tf_op jit(solution)/shard_map/ppermute | solution.py:25
  31.5 3.7 fusion.5
  36.8 4.7 %collective-permute-start.6 = (f32[137,4,128]{2,0,1:T(8,128)S(1)}, f32[137,4,128]{2,0,1:T(8,128)}, u32[]{:S(2)}, u32[]{:S(2)}) collective-permute-start(f32[137,4,128]{2,0,1:T(8,128)S(1)} %convolution_bitcast_fusion.13), channel_id=1, source_target_pairs={{0,1},{1,2},{2,3},{4,5},{5,6},{6,7},{8,9},{9,10},{10,11},{12,13},{... | collective-permute-start | bytes 841736 | tf_op jit(solution)/shard_map/ppermute | solution.py:16
  42.8 8.2 %collective-permute-done.5 = f32[137,8,128]{2,1,0:T(8,128)S(1)} collective-permute-done((f32[137,8,128]{2,1,0:T(8,128)S(1)}, f32[137,8,128]{2,1,0:T(8,128)S(1)}, u32[]{:S(2)}, u32[]{:S(2)}) %collective-permute-start.5) | collective-permute-done | bytes 561184 | tf_op jit(solution)/shard_map/ppermute | solution.py:25
  53.0 3.3 fusion.139
  56.5 2.6 collective-permute-start.9
  59.1 7.2 %collective-permute-done.8 = f32[137,4,32]{2,0,1:T(8,128)S(1)} collective-permute-done((f32[137,4,32]{2,0,1:T(8,128)S(1)}, f32[137,4,32]{2,0,1:T(8,128)S(1)}, u32[]{:S(2)}, u32[]{:S(2)}) %collective-permute-start.8) | collective-permute-done | bytes 70176 | tf_op jit(solution)/shard_map/ppermute | solution.py:16
  67.4 2.6 collective-permute-start.11
  70.0 7.1 %collective-permute-done.10 = f32[137,4,32]{2,0,1:T(8,128)S(1)} collective-permute-done((f32[137,4,32]{2,0,1:T(8,128)S(1)}, f32[137,4,32]{2,0,1:T(8,128)S(1)}, u32[]{:S(2)}, u32[]{:S(2)}) %collective-permute-start.10) | collective-permute-done | bytes 70176 | tf_op jit(solution)/shard_map/ppermute | solution.py:16
  78.2 5.1 %collective-permute-start.13 = (f32[137,4,128]{2,0,1:T(8,128)S(1)}, f32[137,4,128]{2,0,1:T(8,128)}, u32[]{:S(2)}, u32[]{:S(2)}) collective-permute-start(f32[137,4,128]{2,0,1:T(8,128)S(1)} %convolution_bitcast_fusion.11), channel_id=1, source_target_pairs={{0,1},{1,2},{2,3},{4,5},{5,6},{6,7},{8,9},{9,10},{10,11},{12,13},{... | collective-permute-start | bytes 841736 | tf_op jit(solution)/shard_map/ppermute | solution.py:16
  84.9 6.2 %collective-permute-done.12 = f32[137,8,128]{2,1,0:T(8,128)S(1)} collective-permute-done((f32[137,8,128]{2,1,0:T(8,128)S(1)}, f32[137,8,128]{2,1,0:T(8,128)S(1)}, u32[]{:S(2)}, u32[]{:S(2)}) %collective-permute-start.12) | collective-permute-done | bytes 561184 | tf_op jit(solution)/shard_map/ppermute | solution.py:25
  94.7 3.7 fusion.4
  100.3 6.2 %collective-permute-start.16 = (f32[137,4,128]{2,0,1:T(8,128)S(1)}, f32[137,4,128]{2,0,1:T(8,128)}, u32[]{:S(2)}, u32[]{:S(2)}) collective-permute-start(f32[137,4,128]{2,0,1:T(8,128)S(1)} %convolution_bitcast_fusion.9), channel_id=1, source_target_pairs={{0,1},{1,2},{2,3},{4,5},{5,6},{6,7},{8,9},{9,10},{10,11},{12,13},{... | collective-permute-start | bytes 841736 | tf_op jit(solution)/shard_map/ppermute | solution.py:16
  107.8 4.7 %collective-permute-done.15 = f32[137,8,128]{2,1,0:T(8,128)S(1)} collective-permute-done((f32[137,8,128]{2,1,0:T(8,128)S(1)}, f32[137,8,128]{2,1,0:T(8,128)S(1)}, u32[]{:S(2)}, u32[]{:S(2)}) %collective-permute-start.15) | collective-permute-done | bytes 561184 | tf_op jit(solution)/shard_map/ppermute | solution.py:25
  114.4 1.7 collective-permute-done.17
  117.1 3.2 fusion.111
  120.5 2.6 collective-permute-start.19
  124.0 6.3 %collective-permute-done.18 = f32[137,4,32]{2,0,1:T(8,128)S(1)} collective-permute-done((f32[137,4,32]{2,0,1:T(8,128)S(1)}, f32[137,4,32]{2,0,1:T(8,128)S(1)}, u32[]{:S(2)}, u32[]{:S(2)}) %collective-permute-start.18) | collective-permute-done | bytes 70176 | tf_op jit(solution)/shard_map/ppermute | solution.py:16
  130.3 1.5 multiply_reduce_fusion.6
  131.8 10.4 %all-reduce.3 = (f32[]{:T(128)}, f32[]{:T(128)}, f32[]{:T(128)}) all-reduce(f32[]{:T(128)} %get-tuple-element.18, f32[]{:T(128)} %get-tuple-element.19, f32[]{:T(128)} %multiply_reduce_fusion.7), channel_id=1, replica_groups=mesh['lon'=8,'lat'=4] {'lat'}, use_global_device_ids=true, to_apply=%region_11.13 | all-reduce | flops 3 | bytes 24 | tf_op jit(solution)/shard_map/psum | solution.py:118
  142.1 13.2 %all-reduce.1 = (f32[]{:T(128)}, f32[]{:T(128)}, f32[]{:T(128)}) all-reduce(f32[]{:T(128)} %get-tuple-element.29, f32[]{:T(128)} %get-tuple-element.30, f32[]{:T(128)} %get-tuple-element.31), channel_id=1, replica_groups=mesh['lon'=8,'lat'=4] {'lon'}, use_global_device_ids=true, to_apply=%region_12.14 | all-reduce | flops 3 | bytes 24 | tf_op jit(solution)/shard_map/psum | solution.py:118
  158.1 39.1 %psum.98 = f32[]{:T(128)} all-reduce(f32[]{:T(128)} %get-tuple-element.17), channel_id=1, replica_groups=mesh['lon'=8,'lat'=4] {'lon','lat'}, use_global_device_ids=true, to_apply=%region_3.5 | all-reduce | flops 1 | bytes 8 | tf_op jit(solution)/shard_map/psum | solution.py:125
  202.9 2.6 collective-permute-start.21
  205.6 4.4 %collective-permute-done.20 = f32[137,4,32]{2,0,1:T(8,128)S(1)} collective-permute-done((f32[137,4,32]{2,0,1:T(8,128)S(1)}, f32[137,4,32]{2,0,1:T(8,128)S(1)}, u32[]{:S(2)}, u32[]{:S(2)}) %collective-permute-start.20) | collective-permute-done | bytes 70176 | tf_op jit(solution)/shard_map/ppermute | solution.py:16
  210.0 2.1 collective-permute-done.21
  212.0 1.5 convolution_bitcast_fusion.7
  214.8 3.2 collective-permute-start.22
  218.0 4.1 collective-permute-start.23
  223.4 8.1 %collective-permute-done.22 = f32[137,8,128]{2,1,0:T(8,128)S(1)} collective-permute-done((f32[137,8,128]{2,1,0:T(8,128)S(1)}, f32[137,8,128]{2,1,0:T(8,128)S(1)}, u32[]{:S(2)}, u32[]{:S(2)}) %collective-permute-start.22) | collective-permute-done | bytes 561184 | tf_op jit(solution)/shard_map/ppermute | solution.py:25
  234.5 5.1 %fusion.3 = f32[137,4,128]{2,0,1:T(8,128)S(1)} fusion(f32[137,4,128]{2,0,1:T(8,128)S(1)} %reverse_select_fusion.6, f32[137,4,128]{2,0,1:T(8,128)S(1)} %reverse_select_fusion.7, f32[137,4,128]{2,0,1:T(8,128)} %convolution_bitcast_fusion.7, f32[137,4,128]{2,1,0:T(4,128)S(1)} %copy-done.6, f32[137,137]{1,0:T(8,128)S(1)} %copy-done, f32[]{:T(128)} %bitcast.9, ...), kind=kOutput, calls=%fused_computation.19 | convolution fusion | flops 116719616 | bytes 1477976 | tf_op jit(solution)/shard_map/kl,lji->kji/dot_general | solution.py:100
  240.8 5.0 %collective-permute-start.26 = (f32[137,4,128]{2,0,1:T(8,128)S(1)}, f32[137,4,128]{2,0,1:T(8,128)}, u32[]{:S(2)}, u32[]{:S(2)}) collective-permute-start(f32[137,4,128]{2,0,1:T(8,128)S(1)} %convolution_bitcast_fusion.5), channel_id=1, source_target_pairs={{0,1},{1,2},{2,3},{4,5},{5,6},{6,7},{8,9},{9,10},{10,11},{12,13},{... | collective-permute-start | bytes 841736 | tf_op jit(solution)/shard_map/ppermute | solution.py:16
  245.8 1.5 collective-permute-start.27
  247.3 7.9 %collective-permute-done.25 = f32[137,8,128]{2,1,0:T(8,128)S(1)} collective-permute-done((f32[137,8,128]{2,1,0:T(8,128)S(1)}, f32[137,8,128]{2,1,0:T(8,128)S(1)}, u32[]{:S(2)}, u32[]{:S(2)}) %collective-permute-start.25) | collective-permute-done | bytes 561184 | tf_op jit(solution)/shard_map/ppermute | solution.py:25
  255.8 1.7 gather_fusion.5
  257.5 1.6 copy.216
  260.3 3.2 fusion.83
  263.7 2.6 collective-permute-start.29
  266.4 6.5 %collective-permute-done.28 = f32[137,4,32]{2,0,1:T(8,128)S(1)} collective-permute-done((f32[137,4,32]{2,0,1:T(8,128)S(1)}, f32[137,4,32]{2,0,1:T(8,128)S(1)}, u32[]{:S(2)}, u32[]{:S(2)}) %collective-permute-start.28) | collective-permute-done | bytes 70176 | tf_op jit(solution)/shard_map/ppermute | solution.py:16
  273.9 2.6 collective-permute-start.31
  276.6 7.4 %collective-permute-done.30 = f32[137,4,32]{2,0,1:T(8,128)S(1)} collective-permute-done((f32[137,4,32]{2,0,1:T(8,128)S(1)}, f32[137,4,32]{2,0,1:T(8,128)S(1)}, u32[]{:S(2)}, u32[]{:S(2)}) %collective-permute-start.30) | collective-permute-done | bytes 70176 | tf_op jit(solution)/shard_map/ppermute | solution.py:16
  285.1 5.9 %collective-permute-start.33 = (f32[137,4,128]{2,0,1:T(8,128)S(1)}, f32[137,4,128]{2,0,1:T(8,128)}, u32[]{:S(2)}, u32[]{:S(2)}) collective-permute-start(f32[137,4,128]{2,0,1:T(8,128)S(1)} %convolution_bitcast_fusion.3), channel_id=1, source_target_pairs={{0,1},{1,2},{2,3},{4,5},{5,6},{6,7},{8,9},{9,10},{10,11},{12,13},{... | collective-permute-start | bytes 841736 | tf_op jit(solution)/shard_map/ppermute | solution.py:16
  292.3 6.4 %collective-permute-done.32 = f32[137,8,128]{2,1,0:T(8,128)} collective-permute-done((f32[137,8,128]{2,1,0:T(8,128)S(1)}, f32[137,8,128]{2,1,0:T(8,128)}, u32[]{:S(2)}, u32[]{:S(2)}) %collective-permute-start.32) | collective-permute-done | bytes 561184 | tf_op jit(solution)/shard_map/ppermute | solution.py:25
  298.6 1.6 copy.220
  300.2 1.7 gather_fusion.6
  302.0 1.6 copy.221
  304.6 3.7 fusion.2
  309.1 1.8 collective-permute-start.35
  310.9 6.0 %collective-permute-start.36 = (f32[137,4,128]{2,0,1:T(8,128)S(1)}, f32[137,4,128]{2,0,1:T(8,128)}, u32[]{:S(2)}, u32[]{:S(2)}) collective-permute-start(f32[137,4,128]{2,0,1:T(8,128)S(1)} %convolution_bitcast_fusion.1), channel_id=1, source_target_pairs={{0,1},{1,2},{2,3},{4,5},{5,6},{6,7},{8,9},{9,10},{10,11},{12,13},{... | collective-permute-start | bytes 841736 | tf_op jit(solution)/shard_map/ppermute | solution.py:16
  318.2 5.4 %collective-permute-done.35 = f32[137,8,128]{2,1,0:T(8,128)} collective-permute-done((f32[137,8,128]{2,1,0:T(8,128)S(1)}, f32[137,8,128]{2,1,0:T(8,128)}, u32[]{:S(2)}, u32[]{:S(2)}) %collective-permute-start.35) | collective-permute-done | bytes 561184 | tf_op jit(solution)/shard_map/ppermute | solution.py:25
  323.7 1.6 copy.225
  325.2 1.7 gather_fusion.7
  327.0 1.6 copy.226
  328.8 3.2 fusion.55
  332.2 2.6 collective-permute-start.39
  334.8 7.3 %collective-permute-done.38 = f32[137,4,32]{2,0,1:T(8,128)S(1)} collective-permute-done((f32[137,4,32]{2,0,1:T(8,128)S(1)}, f32[137,4,32]{2,0,1:T(8,128)S(1)}, u32[]{:S(2)}, u32[]{:S(2)}) %collective-permute-start.38) | collective-permute-done | bytes 70176 | tf_op jit(solution)/shard_map/ppermute | solution.py:16
  342.1 1.5 multiply_reduce_fusion.3
  343.6 13.5 %all-reduce.2 = (f32[]{:T(128)}, f32[]{:T(128)}, f32[]{:T(128)}) all-reduce(f32[]{:T(128)} %get-tuple-element.14, f32[]{:T(128)} %get-tuple-element.16, f32[]{:T(128)} %get-tuple-element.15), channel_id=1, replica_groups=mesh['lon'=8,'lat'=4] {'lat'}, use_global_device_ids=true, to_apply=%region_22.24 | all-reduce | flops 3 | bytes 24 | tf_op jit(solution)/shard_map/psum | solution.py:118
  357.1 12.5 %all-reduce = (f32[]{:T(128)}, f32[]{:T(128)}, f32[]{:T(128)}) all-reduce(f32[]{:T(128)} %get-tuple-element.26, f32[]{:T(128)} %get-tuple-element.27, f32[]{:T(128)} %get-tuple-element.28), channel_id=1, replica_groups=mesh['lon'=8,'lat'=4] {'lon'}, use_global_device_ids=true, to_apply=%region_23.25 | all-reduce | flops 3 | bytes 24 | tf_op jit(solution)/shard_map/psum | solution.py:118
  371.9 37.7 %psum.105 = f32[]{:T(128)} all-reduce(f32[]{:T(128)} %get-tuple-element.13), channel_id=1, replica_groups=mesh['lon'=8,'lat'=4] {'lon','lat'}, use_global_device_ids=true, to_apply=%region_14.16 | all-reduce | flops 1 | bytes 8 | tf_op jit(solution)/shard_map/psum | solution.py:125
  (161 shorter events, 46.6 us)
Async XLA Ops:
  0.6 30.1 %copy-start = (f32[137,137]{1,0:T(8,128)S(1)}, f32[137,137]{1,0:T(8,128)}, u32[]{:S(2)}) copy-start(f32[137,137]{1,0:T(8,128)} %param.15) | copy-start | bytes 225232
  0.6 4.6 %copy-start.3 = (s32[4]{0:T(128)S(1)}, s32[4]{0:T(128)}, u32[]{:S(2)}) copy-start(s32[4]{0:T(128)} %param.11) | copy-start | bytes 52
  0.7 4.6 %copy-start.2 = (f32[4,33]{1,0:T(4,128)S(1)}, f32[4,33]{1,0:T(4,128)}, u32[]{:S(2)}) copy-start(f32[4,33]{1,0:T(4,128)} %param.12) | copy-start | bytes 1588
  0.7 5.2 %copy-start.9 = (f32[5]{0:T(128)S(1)}, f32[5]{0:T(128)}, u32[]{:S(2)}) copy-start(f32[5]{0:T(128)} %param.14) | copy-start | bytes 64
  1.8 8.3 %collective-permute-start = (f32[137,4,32]{2,0,1:T(8,128)S(1)}, f32[137,4,32]{2,0,1:T(8,128)S(1)}, u32[]{:S(2)}, u32[]{:S(2)}) collective-permute-start(f32[137,4,32]{2,0,1:T(8,128)S(1)} %get-tuple-element.66), channel_id=1, source_target_pairs={{0,4},{4,8},{8,12},{12,16},{16,20},{20,24},{24,28},{28,0},{1,5},{5... | collective-permute-start | bytes 210440 | tf_op jit(solution)/shard_map/ppermute | solution.py:16
  2.3 9.3 %collective-permute-start.1 = (f32[137,4,32]{2,0,1:T(8,128)S(1)}, f32[137,4,32]{2,0,1:T(8,128)S(1)}, u32[]{:S(2)}, u32[]{:S(2)}) collective-permute-start(f32[137,4,32]{2,0,1:T(8,128)S(1)} %get-tuple-element.67), channel_id=1, source_target_pairs={{4,0},{8,4},{12,8},{16,12},{20,16},{24,20},{28,24},{0,28},{5,1},{9... | collective-permute-start | bytes 210440 | tf_op jit(solution)/shard_map/ppermute | solution.py:19
  12.5 2.9 copy-start.8
  12.7 16.0 %collective-permute-start.2 = (f32[137,8,128]{2,1,0:T(8,128)S(1)}, f32[137,8,128]{2,1,0:T(8,128)S(1)}, u32[]{:S(2)}, u32[]{:S(2)}) collective-permute-start(f32[137,8,128]{2,1,0:T(8,128)S(1)} %copy.185), channel_id=1, source_target_pairs={{0,16},{4,20},{8,24},{12,28},{16,0},{20,4},{24,8},{28,12},{1,17},{... | collective-permute-start | bytes 1683464 | tf_op jit(solution)/shard_map/ppermute | solution.py:25
  16.1 14.5 %collective-permute-start.3 = (f32[137,4,128]{2,0,1:T(8,128)S(1)}, f32[137,4,128]{2,0,1:T(8,128)S(1)}, u32[]{:S(2)}, u32[]{:S(2)}) collective-permute-start(f32[137,4,128]{2,0,1:T(8,128)S(1)} %convolution_bitcast_fusion.15), channel_id=1, source_target_pairs={{0,1},{1,2},{2,3},{4,5},{5,6},{6,7},{8,9},{9,10},{10,11},{12,13},{... | collective-permute-start | bytes 841736 | tf_op jit(solution)/shard_map/ppermute | solution.py:16
  19.6 11.0 %collective-permute-start.4 = (f32[137,4,128]{2,0,1:T(8,128)S(1)}, f32[137,4,128]{2,0,1:T(8,128)S(1)}, u32[]{:S(2)}, u32[]{:S(2)}) collective-permute-start(f32[137,4,128]{2,0,1:T(8,128)S(1)} %convolution_bitcast_fusion.15), channel_id=1, source_target_pairs={{1,0},{2,1},{3,2},{5,4},{6,5},{7,6},{9,8},{10,9},{11,10},{13,12},{... | collective-permute-start | bytes 841736 | tf_op jit(solution)/shard_map/ppermute | solution.py:19
  30.6 1.0 copy-start.4
  36.0 15.0 %collective-permute-start.5 = (f32[137,8,128]{2,1,0:T(8,128)S(1)}, f32[137,8,128]{2,1,0:T(8,128)S(1)}, u32[]{:S(2)}, u32[]{:S(2)}) collective-permute-start(f32[137,8,128]{2,1,0:T(8,128)S(1)} %copy.190), channel_id=1, source_target_pairs={{0,16},{4,20},{8,24},{12,28},{16,0},{20,4},{24,8},{28,12},{1,17},{... | collective-permute-start | bytes 1683464 | tf_op jit(solution)/shard_map/ppermute | solution.py:25
  36.8 16.1 %collective-permute-start.6 = (f32[137,4,128]{2,0,1:T(8,128)S(1)}, f32[137,4,128]{2,0,1:T(8,128)}, u32[]{:S(2)}, u32[]{:S(2)}) collective-permute-start(f32[137,4,128]{2,0,1:T(8,128)S(1)} %convolution_bitcast_fusion.13), channel_id=1, source_target_pairs={{0,1},{1,2},{2,3},{4,5},{5,6},{6,7},{8,9},{9,10},{10,11},{12,13},{... | collective-permute-start | bytes 841736 | tf_op jit(solution)/shard_map/ppermute | solution.py:16
  41.5 11.4 %collective-permute-start.7 = (f32[137,4,128]{2,0,1:T(8,128)S(1)}, f32[137,4,128]{2,0,1:T(8,128)S(1)}, u32[]{:S(2)}, u32[]{:S(2)}) collective-permute-start(f32[137,4,128]{2,0,1:T(8,128)S(1)} %convolution_bitcast_fusion.13), channel_id=1, source_target_pairs={{1,0},{2,1},{3,2},{5,4},{6,5},{7,6},{9,8},{10,9},{11,10},{13,12},{... | collective-permute-start | bytes 841736 | tf_op jit(solution)/shard_map/ppermute | solution.py:19
  53.0 13.3 %copy-start.1 = (f32[137,4,128]{2,1,0:T(4,128)S(1)}, f32[137,4,128]{2,1,0:T(4,128)}, u32[]{:S(2)}) copy-start(f32[137,4,128]{2,1,0:T(4,128)} %param.9) | copy-start | bytes 841732
  56.4 9.9 %collective-permute-start.8 = (f32[137,4,32]{2,0,1:T(8,128)S(1)}, f32[137,4,32]{2,0,1:T(8,128)S(1)}, u32[]{:S(2)}, u32[]{:S(2)}) collective-permute-start(f32[137,4,32]{2,0,1:T(8,128)S(1)} %get-tuple-element.64), channel_id=1, source_target_pairs={{0,4},{4,8},{8,12},{12,16},{16,20},{20,24},{24,28},{28,0},{1,5},{5... | collective-permute-start | bytes 210440 | tf_op jit(solution)/shard_map/ppermute | solution.py:16
  56.5 9.8 %collective-permute-start.9 = (f32[137,4,32]{2,0,1:T(8,128)S(1)}, f32[137,4,32]{2,0,1:T(8,128)S(1)}, u32[]{:S(2)}, u32[]{:S(2)}) collective-permute-start(f32[137,4,32]{2,0,1:T(8,128)S(1)} %get-tuple-element.65), channel_id=1, source_target_pairs={{4,0},{8,4},{12,8},{16,12},{20,16},{24,20},{28,24},{0,28},{5,1},{9... | collective-permute-start | bytes 210440 | tf_op jit(solution)/shard_map/ppermute | solution.py:19
  67.3 9.8 %collective-permute-start.10 = (f32[137,4,32]{2,0,1:T(8,128)S(1)}, f32[137,4,32]{2,0,1:T(8,128)S(1)}, u32[]{:S(2)}, u32[]{:S(2)}) collective-permute-start(f32[137,4,32]{2,0,1:T(8,128)S(1)} %get-tuple-element.62), channel_id=1, source_target_pairs={{0,4},{4,8},{8,12},{12,16},{16,20},{20,24},{24,28},{28,0},{1,5},{5... | collective-permute-start | bytes 210440 | tf_op jit(solution)/shard_map/ppermute | solution.py:16
  67.4 9.7 %collective-permute-start.11 = (f32[137,4,32]{2,0,1:T(8,128)S(1)}, f32[137,4,32]{2,0,1:T(8,128)S(1)}, u32[]{:S(2)}, u32[]{:S(2)}) collective-permute-start(f32[137,4,32]{2,0,1:T(8,128)S(1)} %get-tuple-element.63), channel_id=1, source_target_pairs={{4,0},{8,4},{12,8},{16,12},{20,16},{24,20},{28,24},{0,28},{5,1},{9... | collective-permute-start | bytes 210440 | tf_op jit(solution)/shard_map/ppermute | solution.py:19
  78.2 12.9 %collective-permute-start.12 = (f32[137,8,128]{2,1,0:T(8,128)S(1)}, f32[137,8,128]{2,1,0:T(8,128)S(1)}, u32[]{:S(2)}, u32[]{:S(2)}) collective-permute-start(f32[137,8,128]{2,1,0:T(8,128)S(1)} %copy.196), channel_id=1, source_target_pairs={{0,16},{4,20},{8,24},{12,28},{16,0},{20,4},{24,8},{28,12},{1,17},{... | collective-permute-start | bytes 1683464 | tf_op jit(solution)/shard_map/ppermute | solution.py:25
  78.2 14.7 %collective-permute-start.13 = (f32[137,4,128]{2,0,1:T(8,128)S(1)}, f32[137,4,128]{2,0,1:T(8,128)}, u32[]{:S(2)}, u32[]{:S(2)}) collective-permute-start(f32[137,4,128]{2,0,1:T(8,128)S(1)} %convolution_bitcast_fusion.11), channel_id=1, source_target_pairs={{0,1},{1,2},{2,3},{4,5},{5,6},{6,7},{8,9},{9,10},{10,11},{12,13},{... | collective-permute-start | bytes 841736 | tf_op jit(solution)/shard_map/ppermute | solution.py:16
  83.4 10.3 %collective-permute-start.14 = (f32[137,4,128]{2,0,1:T(8,128)S(1)}, f32[137,4,128]{2,0,1:T(8,128)}, u32[]{:S(2)}, u32[]{:S(2)}) collective-permute-start(f32[137,4,128]{2,0,1:T(8,128)S(1)} %convolution_bitcast_fusion.11), channel_id=1, source_target_pairs={{1,0},{2,1},{3,2},{5,4},{6,5},{7,6},{9,8},{10,9},{11,10},{13,12},{... | collective-permute-start | bytes 841736 | tf_op jit(solution)/shard_map/ppermute | solution.py:19
  92.9 1.8 copy-start.5
  99.2 13.2 %collective-permute-start.15 = (f32[137,8,128]{2,1,0:T(8,128)S(1)}, f32[137,8,128]{2,1,0:T(8,128)S(1)}, u32[]{:S(2)}, u32[]{:S(2)}) collective-permute-start(f32[137,8,128]{2,1,0:T(8,128)S(1)} %copy.201), channel_id=1, source_target_pairs={{0,16},{4,20},{8,24},{12,28},{16,0},{20,4},{24,8},{28,12},{1,17},{... | collective-permute-start | bytes 1683464 | tf_op jit(solution)/shard_map/ppermute | solution.py:25
  100.3 14.0 %collective-permute-start.16 = (f32[137,4,128]{2,0,1:T(8,128)S(1)}, f32[137,4,128]{2,0,1:T(8,128)}, u32[]{:S(2)}, u32[]{:S(2)}) collective-permute-start(f32[137,4,128]{2,0,1:T(8,128)S(1)} %convolution_bitcast_fusion.9), channel_id=1, source_target_pairs={{0,1},{1,2},{2,3},{4,5},{5,6},{6,7},{8,9},{9,10},{10,11},{12,13},{... | collective-permute-start | bytes 841736 | tf_op jit(solution)/shard_map/ppermute | solution.py:16
  106.5 9.6 %collective-permute-start.17 = (f32[137,4,128]{2,0,1:T(8,128)S(1)}, f32[137,4,128]{2,0,1:T(8,128)}, u32[]{:S(2)}, u32[]{:S(2)}) collective-permute-start(f32[137,4,128]{2,0,1:T(8,128)S(1)} %convolution_bitcast_fusion.9), channel_id=1, source_target_pairs={{1,0},{2,1},{3,2},{5,4},{6,5},{7,6},{9,8},{10,9},{11,10},{13,12},{... | collective-permute-start | bytes 841736 | tf_op jit(solution)/shard_map/ppermute | solution.py:19
  120.5 9.8 %collective-permute-start.18 = (f32[137,4,32]{2,0,1:T(8,128)S(1)}, f32[137,4,32]{2,0,1:T(8,128)S(1)}, u32[]{:S(2)}, u32[]{:S(2)}) collective-permute-start(f32[137,4,32]{2,0,1:T(8,128)S(1)} %get-tuple-element.60), channel_id=1, source_target_pairs={{0,4},{4,8},{8,12},{12,16},{16,20},{20,24},{24,28},{28,0},{1,5},{5... | collective-permute-start | bytes 210440 | tf_op jit(solution)/shard_map/ppermute | solution.py:16
  120.5 9.7 %collective-permute-start.19 = (f32[137,4,32]{2,0,1:T(8,128)S(1)}, f32[137,4,32]{2,0,1:T(8,128)S(1)}, u32[]{:S(2)}, u32[]{:S(2)}) collective-permute-start(f32[137,4,32]{2,0,1:T(8,128)S(1)} %get-tuple-element.61), channel_id=1, source_target_pairs={{4,0},{8,4},{12,8},{16,12},{20,16},{24,20},{28,24},{0,28},{5,1},{9... | collective-permute-start | bytes 210440 | tf_op jit(solution)/shard_map/ppermute | solution.py:19
  202.9 7.1 %collective-permute-start.20 = (f32[137,4,32]{2,0,1:T(8,128)S(1)}, f32[137,4,32]{2,0,1:T(8,128)S(1)}, u32[]{:S(2)}, u32[]{:S(2)}) collective-permute-start(f32[137,4,32]{2,0,1:T(8,128)S(1)} %get-tuple-element.58), channel_id=1, source_target_pairs={{0,4},{4,8},{8,12},{12,16},{16,20},{20,24},{24,28},{28,0},{1,5},{5... | collective-permute-start | bytes 210440 | tf_op jit(solution)/shard_map/ppermute | solution.py:16
  202.9 9.1 %collective-permute-start.21 = (f32[137,4,32]{2,0,1:T(8,128)S(1)}, f32[137,4,32]{2,0,1:T(8,128)S(1)}, u32[]{:S(2)}, u32[]{:S(2)}) collective-permute-start(f32[137,4,32]{2,0,1:T(8,128)S(1)} %get-tuple-element.59), channel_id=1, source_target_pairs={{4,0},{8,4},{12,8},{16,12},{20,16},{24,20},{28,24},{0,28},{5,1},{9... | collective-permute-start | bytes 210440 | tf_op jit(solution)/shard_map/ppermute | solution.py:19
  214.8 16.7 %collective-permute-start.22 = (f32[137,8,128]{2,1,0:T(8,128)S(1)}, f32[137,8,128]{2,1,0:T(8,128)S(1)}, u32[]{:S(2)}, u32[]{:S(2)}) collective-permute-start(f32[137,8,128]{2,1,0:T(8,128)S(1)} %copy.209), channel_id=1, source_target_pairs={{0,16},{4,20},{8,24},{12,28},{16,0},{20,4},{24,8},{28,12},{1,17},{... | collective-permute-start | bytes 1683464 | tf_op jit(solution)/shard_map/ppermute | solution.py:25
  218.0 15.4 %collective-permute-start.23 = (f32[137,4,128]{2,0,1:T(8,128)}, f32[137,4,128]{2,0,1:T(8,128)}, u32[]{:S(2)}, u32[]{:S(2)}) collective-permute-start(f32[137,4,128]{2,0,1:T(8,128)} %convolution_bitcast_fusion.7), channel_id=1, source_target_pairs={{0,1},{1,2},{2,3},{4,5},{5,6},{6,7},{8,9},{9,10},{10,11},{12,13},{... | collective-permute-start | bytes 841736 | tf_op jit(solution)/shard_map/ppermute | solution.py:16
  222.1 11.4 %collective-permute-start.24 = (f32[137,4,128]{2,0,1:T(8,128)}, f32[137,4,128]{2,0,1:T(8,128)}, u32[]{:S(2)}, u32[]{:S(2)}) collective-permute-start(f32[137,4,128]{2,0,1:T(8,128)} %convolution_bitcast_fusion.7), channel_id=1, source_target_pairs={{1,0},{2,1},{3,2},{5,4},{6,5},{7,6},{9,8},{10,9},{11,10},{13,12},{... | collective-permute-start | bytes 841736 | tf_op jit(solution)/shard_map/ppermute | solution.py:19
  233.4 1.1 copy-start.6
  240.4 14.8 %collective-permute-start.25 = (f32[137,8,128]{2,1,0:T(8,128)S(1)}, f32[137,8,128]{2,1,0:T(8,128)S(1)}, u32[]{:S(2)}, u32[]{:S(2)}) collective-permute-start(f32[137,8,128]{2,1,0:T(8,128)S(1)} %copy.214), channel_id=1, source_target_pairs={{0,16},{4,20},{8,24},{12,28},{16,0},{20,4},{24,8},{28,12},{1,17},{... | collective-permute-start | bytes 1683464 | tf_op jit(solution)/shard_map/ppermute | solution.py:25
  240.8 18.4 %collective-permute-start.26 = (f32[137,4,128]{2,0,1:T(8,128)S(1)}, f32[137,4,128]{2,0,1:T(8,128)}, u32[]{:S(2)}, u32[]{:S(2)}) collective-permute-start(f32[137,4,128]{2,0,1:T(8,128)S(1)} %convolution_bitcast_fusion.5), channel_id=1, source_target_pairs={{0,1},{1,2},{2,3},{4,5},{5,6},{6,7},{8,9},{9,10},{10,11},{12,13},{... | collective-permute-start | bytes 841736 | tf_op jit(solution)/shard_map/ppermute | solution.py:16
  245.8 13.5 %collective-permute-start.27 = (f32[137,4,128]{2,0,1:T(8,128)S(1)}, f32[137,4,128]{2,0,1:T(8,128)}, u32[]{:S(2)}, u32[]{:S(2)}) collective-permute-start(f32[137,4,128]{2,0,1:T(8,128)S(1)} %convolution_bitcast_fusion.5), channel_id=1, source_target_pairs={{1,0},{2,1},{3,2},{5,4},{6,5},{7,6},{9,8},{10,9},{11,10},{13,12},{... | collective-permute-start | bytes 841736 | tf_op jit(solution)/shard_map/ppermute | solution.py:19
  263.7 9.2 %collective-permute-start.28 = (f32[137,4,32]{2,0,1:T(8,128)S(1)}, f32[137,4,32]{2,0,1:T(8,128)S(1)}, u32[]{:S(2)}, u32[]{:S(2)}) collective-permute-start(f32[137,4,32]{2,0,1:T(8,128)S(1)} %get-tuple-element.56), channel_id=1, source_target_pairs={{0,4},{4,8},{8,12},{12,16},{16,20},{20,24},{24,28},{28,0},{1,5},{5... | collective-permute-start | bytes 210440 | tf_op jit(solution)/shard_map/ppermute | solution.py:16
  263.7 9.2 %collective-permute-start.29 = (f32[137,4,32]{2,0,1:T(8,128)S(1)}, f32[137,4,32]{2,0,1:T(8,128)S(1)}, u32[]{:S(2)}, u32[]{:S(2)}) collective-permute-start(f32[137,4,32]{2,0,1:T(8,128)S(1)} %get-tuple-element.57), channel_id=1, source_target_pairs={{4,0},{8,4},{12,8},{16,12},{20,16},{24,20},{28,24},{0,28},{5,1},{9... | collective-permute-start | bytes 210440 | tf_op jit(solution)/shard_map/ppermute | solution.py:19
  273.9 10.1 %collective-permute-start.30 = (f32[137,4,32]{2,0,1:T(8,128)S(1)}, f32[137,4,32]{2,0,1:T(8,128)S(1)}, u32[]{:S(2)}, u32[]{:S(2)}) collective-permute-start(f32[137,4,32]{2,0,1:T(8,128)S(1)} %get-tuple-element.54), channel_id=1, source_target_pairs={{0,4},{4,8},{8,12},{12,16},{16,20},{20,24},{24,28},{28,0},{1,5},{5... | collective-permute-start | bytes 210440 | tf_op jit(solution)/shard_map/ppermute | solution.py:16
  273.9 10.0 %collective-permute-start.31 = (f32[137,4,32]{2,0,1:T(8,128)S(1)}, f32[137,4,32]{2,0,1:T(8,128)S(1)}, u32[]{:S(2)}, u32[]{:S(2)}) collective-permute-start(f32[137,4,32]{2,0,1:T(8,128)S(1)} %get-tuple-element.55), channel_id=1, source_target_pairs={{4,0},{8,4},{12,8},{16,12},{20,16},{24,20},{28,24},{0,28},{5,1},{9... | collective-permute-start | bytes 210440 | tf_op jit(solution)/shard_map/ppermute | solution.py:19
  285.0 13.6 %collective-permute-start.32 = (f32[137,8,128]{2,1,0:T(8,128)S(1)}, f32[137,8,128]{2,1,0:T(8,128)}, u32[]{:S(2)}, u32[]{:S(2)}) collective-permute-start(f32[137,8,128]{2,1,0:T(8,128)S(1)} %copy.219), channel_id=1, source_target_pairs={{0,16},{4,20},{8,24},{12,28},{16,0},{20,4},{24,8},{28,12},{1,17},{... | collective-permute-start | bytes 1683464 | tf_op jit(solution)/shard_map/ppermute | solution.py:25
  285.1 18.5 %collective-permute-start.33 = (f32[137,4,128]{2,0,1:T(8,128)S(1)}, f32[137,4,128]{2,0,1:T(8,128)}, u32[]{:S(2)}, u32[]{:S(2)}) collective-permute-start(f32[137,4,128]{2,0,1:T(8,128)S(1)} %convolution_bitcast_fusion.3), channel_id=1, source_target_pairs={{0,1},{1,2},{2,3},{4,5},{5,6},{6,7},{8,9},{9,10},{10,11},{12,13},{... | collective-permute-start | bytes 841736 | tf_op jit(solution)/shard_map/ppermute | solution.py:16
  291.0 12.7 %collective-permute-start.34 = (f32[137,4,128]{2,0,1:T(8,128)S(1)}, f32[137,4,128]{2,0,1:T(8,128)S(1)}, u32[]{:S(2)}, u32[]{:S(2)}) collective-permute-start(f32[137,4,128]{2,0,1:T(8,128)S(1)} %convolution_bitcast_fusion.3), channel_id=1, source_target_pairs={{1,0},{2,1},{3,2},{5,4},{6,5},{7,6},{9,8},{10,9},{11,10},{13,12},{... | collective-permute-start | bytes 841736 | tf_op jit(solution)/shard_map/ppermute | solution.py:19
  303.6 1.0 copy-start.7
  309.1 14.6 %collective-permute-start.35 = (f32[137,8,128]{2,1,0:T(8,128)S(1)}, f32[137,8,128]{2,1,0:T(8,128)}, u32[]{:S(2)}, u32[]{:S(2)}) collective-permute-start(f32[137,8,128]{2,1,0:T(8,128)S(1)} %copy.224), channel_id=1, source_target_pairs={{0,16},{4,20},{8,24},{12,28},{16,0},{20,4},{24,8},{28,12},{1,17},{... | collective-permute-start | bytes 1683464 | tf_op jit(solution)/shard_map/ppermute | solution.py:25
  310.9 17.8 %collective-permute-start.36 = (f32[137,4,128]{2,0,1:T(8,128)S(1)}, f32[137,4,128]{2,0,1:T(8,128)}, u32[]{:S(2)}, u32[]{:S(2)}) collective-permute-start(f32[137,4,128]{2,0,1:T(8,128)S(1)} %convolution_bitcast_fusion.1), channel_id=1, source_target_pairs={{0,1},{1,2},{2,3},{4,5},{5,6},{6,7},{8,9},{9,10},{10,11},{12,13},{... | collective-permute-start | bytes 841736 | tf_op jit(solution)/shard_map/ppermute | solution.py:16
  316.9 11.8 %collective-permute-start.37 = (f32[137,4,128]{2,0,1:T(8,128)S(1)}, f32[137,4,128]{2,0,1:T(8,128)S(1)}, u32[]{:S(2)}, u32[]{:S(2)}) collective-permute-start(f32[137,4,128]{2,0,1:T(8,128)S(1)} %convolution_bitcast_fusion.1), channel_id=1, source_target_pairs={{1,0},{2,1},{3,2},{5,4},{6,5},{7,6},{9,8},{10,9},{11,10},{13,12},{... | collective-permute-start | bytes 841736 | tf_op jit(solution)/shard_map/ppermute | solution.py:19
  332.1 10.0 %collective-permute-start.38 = (f32[137,4,32]{2,0,1:T(8,128)S(1)}, f32[137,4,32]{2,0,1:T(8,128)S(1)}, u32[]{:S(2)}, u32[]{:S(2)}) collective-permute-start(f32[137,4,32]{2,0,1:T(8,128)S(1)} %get-tuple-element.52), channel_id=1, source_target_pairs={{0,4},{4,8},{8,12},{12,16},{16,20},{20,24},{24,28},{28,0},{1,5},{5... | collective-permute-start | bytes 210440 | tf_op jit(solution)/shard_map/ppermute | solution.py:16
  332.2 9.9 %collective-permute-start.39 = (f32[137,4,32]{2,0,1:T(8,128)S(1)}, f32[137,4,32]{2,0,1:T(8,128)S(1)}, u32[]{:S(2)}, u32[]{:S(2)}) collective-permute-start(f32[137,4,32]{2,0,1:T(8,128)S(1)} %get-tuple-element.53), channel_id=1, source_target_pairs={{4,0},{8,4},{12,8},{16,12},{20,16},{24,20},{28,24},{0,28},{5,1},{9... | collective-permute-start | bytes 210440 | tf_op jit(solution)/shard_map/ppermute | solution.py:19
